TPU v7x, 128 devices: a whole 4x4x4 slice. The times are simulated.
128 devices in a mesh: dp: 8 (over x, y_hi), seq: 16 (over y_lo, z, core).
Axes of the slice: x: 4, y: 4 (y_hi: 2, y_lo: 2; y = y_hi * 2 + y_lo), z: 4, core: 2. Of those that a mesh axis runs over, the one named last changes fastest.
Arguments:
- caption_states: bfloat16 [8, 128, 4096], P('dp', None, 'seq'), may hold values from -1600 to 1600
- caption_gain: float32 [4096], P('seq'), may hold values from 0.25 to 2.5
- text_proj: bfloat16 [4096, 4608], P('seq'), may hold values from -0.09375 to 0.09375
- caption_len: int32 [8], P('dp'), may hold values from 1 to 128, 640 in all
- slot_source: int32 [8, 128], P('dp'), may hold values from 0 to 127, each once within a row
- query_gain: float32 [128], replicated, may hold values from 0.5 to 2
- key_gain: float32 [128], replicated, may hold values from 0.5 to 2
- image_q: bfloat16 [8, 2048, 1536], P('dp', 'seq'), may hold values from -34 to 34
- image_k: bfloat16 [8, 2048, 1536], P('dp', 'seq'), may hold values from -6.5 to 6.5
- image_v: bfloat16 [8, 2048, 1536], P('dp', 'seq'), may hold values from -6 to 6
- out_weight: bfloat16 [3072, 1536], replicated, may hold values from -0.15625 to 0.15625
- gate: float32 [8, 3072], P('dp'), may hold values from -4 to 4
- d_out: bfloat16 [8, 2048, 3072], P('dp', 'seq'), may hold values from -2.5 to 2.5
Outputs:
- image_out: bfloat16 [8, 2048, 3072], P('dp', 'seq')
- text_attn: bfloat16 [8, 128, 1536], P('dp', 'seq')
- d_attn: bfloat16 [8, 2048, 1536], P('dp', 'seq')
- grad_wo: float32 [3072, 1536], P(('dp', 'seq'))
- grad_gate: float32 [8, 3072], P('dp', 'seq')
Inputs may be any that keep to these rules, and one draw needn't show every extreme that they name: `caption_len`: caption lengths in tokens; the longest is 128. `slot_source`: each row is a permutation: every caption row of the sequence sits in exactly one slot; slots whose row is not below the caption's length are padding.
All inputs are finite; a program needn't handle non-finite values. No bound on the sum of `caption_len` on one device may be relied on, other than what follows from the above.
Results may differ from a plain program's by a relative error of at most 0.0095.
Values may be sent and summed in bfloat16 or wider, within the bound.
A program may use at most 128 MiB of HBM per device.

v0:
```python
import jax
import jax.numpy as jnp
from jax import lax
from jax.sharding import PartitionSpec as P

DT5 = 4096
neg_big = -1e30
eps_norm = 1e-06


def head_norm(values_in, gain_vec):
    shaped = values_in.reshape(values_in.shape[0], -1, gain_vec.shape[0])
    normed = (
        shaped * lax.rsqrt(jnp.mean(shaped * shaped, axis=-1, keepdims=True) + eps_norm) * gain_vec
    )
    return normed.reshape(values_in.shape).astype(jnp.bfloat16)


def text_heads(summed, squares, query_gain, key_gain, inner_width):
    factor = lax.rsqrt(squares / DT5 + eps_norm)
    normed = summed * factor[:, None]
    text_query = head_norm(normed[:, :inner_width], query_gain)
    text_key = head_norm(normed[:, inner_width : 2 * inner_width], key_gain)
    text_value = normed[:, 2 * inner_width :].astype(jnp.bfloat16)
    return (text_query, text_key, text_value)


def start_state(query_heads):
    query_count, head_count, head_size = query_heads.shape
    return (
        jnp.full((head_count, query_count), neg_big, jnp.float32),
        jnp.zeros((head_count, query_count), jnp.float32),
        jnp.zeros((head_count, query_count, head_size), jnp.float32),
    )


def attend(running, query_heads, key_rows, value_rows, usable):
    max_old, total_old, weighted = running
    count_keys = key_rows.shape[0]
    head_size = query_heads.shape[2]
    key_heads = key_rows.reshape(count_keys, -1, head_size)
    value_heads = value_rows.reshape(count_keys, -1, head_size)
    scores = jnp.einsum(
        "qhd,khd->hqk", query_heads, key_heads, preferred_element_type=jnp.float32
    ) * head_size ** (-0.5)
    scores = jnp.where(usable[None, None, :], scores, neg_big)
    max_new = jnp.maximum(max_old, jnp.max(scores, axis=-1))
    weights_now = jnp.where(usable[None, None, :], jnp.exp(scores - max_new[..., None]), 0.0)
    total_new = jnp.sum(weights_now, axis=-1)
    weighted = jnp.einsum(
        "hqk,khd->hqd",
        weights_now.astype(jnp.bfloat16),
        value_heads,
        preferred_element_type=jnp.float32,
    )
    return (max_new, total_new, weighted)


def on_device(
    caption_states,
    caption_gain,
    text_proj,
    caption_len,
    slot_source,
    query_gain,
    key_gain,
    image_q,
    image_k,
    image_v,
    out_weight,
    gate,
    d_out,
):
    seq_count = lax.axis_size("seq")
    seq_index = lax.axis_index("seq")
    slot_total = slot_source.shape[1]
    slot_local = slot_total // seq_count
    image_local = image_q.shape[1]
    inner_width = image_q.shape[2]
    head_size = query_gain.shape[0]
    sources = slot_source[0]
    picked = jnp.take(caption_states[0], sources, axis=0).astype(jnp.float32)
    scaled_rows = (picked * caption_gain).astype(jnp.bfloat16)
    partial_proj = jnp.dot(scaled_rows, text_proj, preferred_element_type=jnp.float32)
    partial_squares = jnp.sum(picked * picked, axis=1)
    usable_slots = sources < caption_len[0]
    own_usable = lax.dynamic_slice_in_dim(usable_slots, seq_index * slot_local, slot_local)
    summed, squares = (
        lax.psum_scatter(partial_proj, "seq", scatter_dimension=0, tiled=True),
        lax.psum_scatter(partial_squares, "seq", scatter_dimension=0, tiled=True),
    )
    text_query, text_key, text_value = text_heads(
        summed, squares, query_gain, key_gain, inner_width
    )
    queries = jnp.concatenate([image_q[0], text_query], axis=0)
    query_heads = queries.reshape(queries.shape[0], -1, head_size)
    key_rows = jnp.concatenate([image_k[0], text_key], axis=0)
    value_rows = jnp.concatenate([image_v[0], text_value], axis=0)
    usable_all = jnp.concatenate(
        [
            jnp.ones((seq_count, image_local), dtype=jnp.bool_),
            usable_slots.reshape(seq_count, slot_local),
        ],
        axis=1,
    ).reshape(-1)
    running = attend(
        start_state(query_heads),
        query_heads,
        lax.all_gather(key_rows, "seq", axis=0, tiled=True),
        lax.all_gather(value_rows, "seq", axis=0, tiled=True),
        usable_all,
    )
    max_final, total_final, weighted = running
    attention = (
        jnp.transpose(weighted / total_final[..., None], (1, 0, 2))
        .reshape(-1, inner_width)
        .astype(jnp.bfloat16)
    )
    image_attn = attention[:image_local]
    text_attn = jnp.where(own_usable[:, None], attention[image_local:], jnp.zeros((), jnp.bfloat16))
    projected = lax.dot_general(
        image_attn, out_weight, (((1,), (1,)), ((), ())), preferred_element_type=jnp.float32
    )
    gate_row = gate[0]
    image_out = (gate_row * projected).astype(jnp.bfloat16)
    cotangent = d_out[0].astype(jnp.float32)
    gated_grad = (gate_row * cotangent).astype(jnp.bfloat16)
    gate_term = jnp.sum(projected * cotangent, axis=0)
    d_attn = jnp.dot(gated_grad, out_weight, preferred_element_type=jnp.float32).astype(
        jnp.bfloat16
    )
    grad_wo = lax.psum_scatter(
        lax.dot_general(
            gated_grad, image_attn, (((0,), (0,)), ((), ())), preferred_element_type=jnp.float32
        ),
        ("dp", "seq"),
        scatter_dimension=0,
        tiled=True,
    )
    grad_gate = lax.psum_scatter(gate_term, "seq", scatter_dimension=0, tiled=True)
    return (image_out[None], text_attn[None], d_attn[None], grad_wo, grad_gate[None])


def solution(mesh):
    in_specs = (
        P("dp", None, "seq"),
        P("seq"),
        P("seq", None),
        P("dp"),
        P("dp", None),
        P(),
        P(),
        P("dp", "seq", None),
        P("dp", "seq", None),
        P("dp", "seq", None),
        P(),
        P("dp", None),
        P("dp", "seq", None),
    )
    out_specs = (
        P("dp", "seq", None),
        P("dp", "seq", None),
        P("dp", "seq", None),
        P(("dp", "seq"), None),
        P("dp", "seq"),
    )
    return jax.shard_map(
        on_device, mesh=mesh, in_specs=in_specs, out_specs=out_specs, check_vma=False
    )
```

profile of v0, /device:TPU:0, one launch (start us, length us, event | category | flops | bytes accessed | tf_op | source)
XLA Modules:
  0.0 446.3 jit_solution(14536937245673772686)
XLA Ops:
  8.1 0.7 fusion.38
  9.5 1.6 gather_fusion
  11.1 2.6 fusion.28
  13.8 1.2 dynamic-slice
  15.9 31.7 %all-reduce.1 = f32[128]{0:T(128)S(1)} all-reduce(f32[128]{0:T(128)S(1)} %fusion.27), channel_id=3, replica_groups=mesh['dp'=8,'seq'=16] {'seq'}, use_global_device_ids=true, to_apply=%region_2.3.clone | all-reduce | flops 128 | bytes 1024
  47.7 0.7 broadcast_bitcast_fusion
  48.3 32.1 %reduce-scatter.3.cloned.1.call-done = f32[8,4608]{1,0:T(8,128)} async-done(((f32[128,4608]{1,0:T(8,128)}), f32[8,4608]{1,0:T(8,128)}) %reduce-scatter.3.cloned.1.call-update) | async-done | bytes 147472 | tf_op jit(solution)/shard_map/reduce_scatter | solution.py:89
  80.4 1.0 broadcast_multiply_fusion
  81.6 1.8 pad_maximum_fusion
  83.5 0.8 pad_maximum_fusion.1
  85.1 40.8 %all-gather.3.cloned.1.call-done = bf16[2176,1536]{1,0:T(8,128)(2,1)} async-done(((bf16[136,1536]{1,0:T(8,128)(2,1)}), bf16[2176,1536]{1,0:T(8,128)(2,1)}) %all-gather.3.cloned.1.call-update) | async-done | bytes 6684688 | tf_op jit(solution)/shard_map/all_gather | solution.py:109
  125.9 9.3 %copy.29 = bf16[2176,1536]{0,1:T(8,128)(2,1)} copy(bf16[2176,1536]{1,0:T(8,128)(2,1)} %all-gather.3.cloned.1.call-done) | data formatting | bytes 13369344 | tf_op jit(solution)/shard_map/all_gather | solution.py:109
  135.3 4.8 %fusion = (f32[12,136]{1,0:T(8,128)S(1)}, f32[12,136,2176]{2,1,0:T(8,128)S(1)}) fusion(pred[2176]{0:T(1024)(128)(4,1)S(1)} %broadcast_in_dim.67, bf16[2176,12,128]{0,2,1:T(8,128)(2,1)} %bitcast.78, bf16[8,12,128]{2,0,1:T(8,128)(2,1)S(1)} %get-tuple-element.9, bf16[128,12,128]{2,0,1:T(8,128)(2,1)S(1)} %copy.28), kind=kOutput, calls=%fused_computation.3 | convolution fusion | flops 920603008 | bytes 21316096 | tf_op jit(solution)/shard_map/qhd,khd->hqk/dot_general | solution.py:43
  140.1 5.1 %copy-done.2 = f32[12,136,2176]{2,1,0:T(8,128)} copy-done((f32[12,136,2176]{2,1,0:T(8,128)}, f32[12,136,2176]{2,1,0:T(8,128)S(1)}, u32[]{:S(2)}) %copy-start.2) | copy-done | bytes 14204952
  145.1 3.8 fusion.1
  148.9 24.5 %all-gather.5.cloned.1.call-done = bf16[2176,1536]{1,0:T(8,128)(2,1)} async-done(((bf16[136,1536]{1,0:T(8,128)(2,1)}), bf16[2176,1536]{1,0:T(8,128)(2,1)}) %all-gather.5.cloned.1.call-update) | async-done | bytes 6684688 | tf_op jit(solution)/shard_map/all_gather | solution.py:110
  173.4 9.4 %copy.31 = bf16[2176,1536]{0,1:T(8,128)(2,1)} copy(bf16[2176,1536]{1,0:T(8,128)(2,1)} %all-gather.5.cloned.1.call-done) | data formatting | bytes 13369344 | tf_op jit(solution)/shard_map/all_gather | solution.py:110
  182.7 10.4 %fusion.15 = bf16[136,12,128]{2,0,1:T(8,128)(2,1)S(1)} fusion(bf16[2176,12,128]{0,2,1:T(8,128)(2,1)} %bitcast.79, f32[12,136,2176]{2,1,0:T(8,128)} %copy-done.2, f32[12,136]{1,0:T(8,128)S(1)} %broadcast_maximum_fusion, pred[2176]{0:T(1024)(128)(4,1)S(1)} %broadcast_in_dim.67, f32[136,12]{0,1:T(8,128)S(1)} %bitcast.89), kind=kOutput, calls=%fused_computation.17 | convolution fusion | flops 927289344 | bytes 21322624 | tf_op jit(solution)/shard_map/hqk,khd->hqd/dot_general | solution.py:50
  193.5 8.0 %fusion.19 = f32[3072,1536]{1,0:T(8,128)} fusion(bf16[128,1536]{0,1:T(8,128)(2,1)S(1)} %bitcast.81, bf16[1,128,3072]{2,1,0:T(8,128)(2,1)S(1)} %copy-done.3, f32[3072]{0:T(1024)S(1)} %bitcast.84), kind=kOutput, calls=%fused_computation.19 | convolution fusion | flops 1209139200 | bytes 20066304 | tf_op jit(solution)/shard_map/dot_general | solution.py:133
  202.4 6.2 %fusion.6 = bf16[1,128,1536]{2,1,0:T(8,128)(2,1)} fusion(bf16[3072,1536]{1,0:T(8,128)(2,1)} %param.23, bf16[1,128,3072]{2,1,0:T(8,128)(2,1)} %param.25, f32[3072]{0:T(1024)S(1)} %bitcast.85), kind=kOutput, calls=%fused_computation.9 | convolution fusion | flops 1209335808 | bytes 10629120 | tf_op jit(solution)/shard_map/dot_general | solution.py:129
  208.8 5.4 %fusion.8 = (f32[3072]{0:T(1024)S(1)}, bf16[1,128,3072]{2,1,0:T(8,128)(2,1)}) fusion(bf16[1,128,3072]{2,1,0:T(8,128)(2,1)} %param.25, f32[3072]{0:T(1024)S(1)} %bitcast.86, bf16[128,1536]{0,1:T(8,128)(2,1)} %bitcast.82, bf16[3072,1536]{1,0:T(8,128)(2,1)S(1)} %bitcast.77), kind=kOutput, calls=%fused_computation.13 | convolution fusion | flops 1209922560 | bytes 11427840 | tf_op jit(solution)/shard_map/dot_general | solution.py:121
  214.2 55.7 %all-reduce.2 = f32[3072]{0:T(1024)S(1)} all-reduce(f32[3072]{0:T(1024)S(1)} %get-tuple-element.7), channel_id=5, replica_groups=mesh['dp'=8,'seq'=16] {'seq'}, use_global_device_ids=true, to_apply=%region_9.10.clone | all-reduce | flops 3072 | bytes 24576
  270.5 1.4 fusion.37
  271.9 167.9 %reduce-scatter.5.cloned.1.call-done = f32[24,1536]{1,0:T(8,128)} async-done(((f32[3072,1536]{1,0:T(8,128)}), f32[24,1536]{1,0:T(8,128)}) %reduce-scatter.5.cloned.1.call-update) | async-done | bytes 147472 | tf_op jit(solution)/shard_map/reduce_scatter | solution.py:132
  (53 shorter events, 3.3 us)
Async XLA Ops:
  7.2 3.9 copy-start
  7.2 77.2 %copy-start.9 = (s32[1,128]{1,0:T(1,128)S(1)}, s32[1,128]{1,0:T(1,128)}, u32[]{:S(2)}) copy-start(s32[1,128]{1,0:T(1,128)} %param.17) | copy-start | bytes 1540
  7.2 76.3 %copy-start.7 = (bf16[1,128,1536]{2,1,0:T(8,128)(2,1)S(1)}, bf16[1,128,1536]{2,1,0:T(8,128)(2,1)}, u32[]{:S(2)}) copy-start(bf16[1,128,1536]{2,1,0:T(8,128)(2,1)} %param.22) | copy-start | bytes 1179652
  7.2 77.4 %copy-start.8 = (bf16[1,128,1536]{2,1,0:T(8,128)(2,1)S(1)}, bf16[1,128,1536]{2,1,0:T(8,128)(2,1)}, u32[]{:S(2)}) copy-start(bf16[1,128,1536]{2,1,0:T(8,128)(2,1)} %param.20) | copy-start | bytes 1179652
  7.2 73.2 %reduce-scatter.3.cloned.1.call-start = ((), (), s32[]{:S(2)}) async-start(), calls=%async_computation.2 | async-start | bytes 2506752 | tf_op jit(solution)/shard_map/reduce_scatter | solution.py:89
  13.7 112.2 %all-gather.3.cloned.1.call-start = ((), (), s32[]{:S(2)}) async-start(), calls=%async_computation.3 | async-start | bytes 7102464 | tf_op jit(solution)/shard_map/all_gather | solution.py:109
  83.4 89.9 %all-gather.5.cloned.1.call-start = ((), (), s32[]{:S(2)}) async-start(), calls=%async_computation.4 | async-start | bytes 7102464 | tf_op jit(solution)/shard_map/all_gather | solution.py:110
  84.3 355.4 %reduce-scatter.5.cloned.1.call-start = ((), (), s32[]{:S(2)}) async-start(), calls=%async_computation.5 | async-start | bytes 19021824 | tf_op jit(solution)/shard_map/reduce_scatter | solution.py:132
  140.1 5.1 %copy-start.2 = (f32[12,136,2176]{2,1,0:T(8,128)}, f32[12,136,2176]{2,1,0:T(8,128)S(1)}, u32[]{:S(2)}) copy-start(f32[12,136,2176]{2,1,0:T(8,128)S(1)} %get-tuple-element.14) | copy-start | bytes 42614788
  182.7 10.7 %copy-start.3 = (bf16[1,128,3072]{2,1,0:T(8,128)(2,1)S(1)}, bf16[1,128,3072]{2,1,0:T(8,128)(2,1)}, u32[]{:S(2)}) copy-start(bf16[1,128,3072]{2,1,0:T(8,128)(2,1)} %param.25) | copy-start | bytes 2359300
  182.7 10.7 %copy-start.6 = (f32[1,3072]{1,0:T(1,128)S(1)}, f32[1,3072]{1,0:T(1,128)}, u32[]{:S(2)}) copy-start(f32[1,3072]{1,0:T(1,128)} %param.24) | copy-start | bytes 36868
  193.2 8.3 %copy-start.5 = (bf16[136,12,128]{2,0,1:T(8,128)(2,1)}, bf16[136,12,128]{2,0,1:T(8,128)(2,1)S(1)}, u32[]{:S(2)}) copy-start(bf16[136,12,128]{2,0,1:T(8,128)(2,1)S(1)} %fusion.15) | copy-start | bytes 1253380
  193.5 8.1 %copy-start.4 = (bf16[128,12,128]{0,2,1:T(8,128)(2,1)}, bf16[128,12,128]{0,2,1:T(8,128)(2,1)S(1)}, u32[]{:S(2)}) copy-start(bf16[128,12,128]{0,2,1:T(8,128)(2,1)S(1)} %copy.33) | copy-start | bytes 1179652
  201.5 7.1 %slice-start = ((s8[9437184]{0:T(1024)(128)(4,1)}), s8[1048576]{0:T(1024)(128)(4,1)S(1)}, s32[]{:S(2)}) async-start(s8[9437184]{0:T(1024)(128)(4,1)} %bitcast.76), calls=%async_computation.6 | async-start | bytes 2097152
  202.4 6.2 %slice-start.1 = ((s8[9437184]{0:T(1024)(128)(4,1)}), s8[4194304]{0:T(1024)(128)(4,1)S(1)}, s32[]{:S(2)}) async-start(s8[9437184]{0:T(1024)(128)(4,1)} %bitcast.76), calls=%async_computation.7 | async-start | bytes 8388608
  202.4 6.4 %slice-start.2 = ((s8[9437184]{0:T(1024)(128)(4,1)}), s8[4194304]{0:T(1024)(128)(4,1)S(1)}, s32[]{:S(2)}) async-start(s8[9437184]{0:T(1024)(128)(4,1)} %bitcast.76), calls=%async_computation.8 | async-start | bytes 8388608
  202.4 237.4 %copy-start.1 = (bf16[256,4608]{1,0:T(8,128)(2,1)S(1)}, bf16[256,4608]{1,0:T(8,128)(2,1)}, u32[]{:S(2)}) copy-start(bf16[256,4608]{1,0:T(8,128)(2,1)} %param.15) | copy-start | bytes 7077892
Sparse Core Ops, SparseCore 0:
  13.9 66.5 reduce-scatter.2
  83.6 42.3 all-gather.2
  128.2 45.1 all-gather.4
  201.7 238.0 reduce-scatter.4
where the time goes:
time: 447 us; the launch traced here: 446 us
  waiting for transfers between devices  265 us (59%)
  blocking collectives  87.4 us (20%)
  matrix products  37.4 us (8%)
  local copies, waits for them, and re-layouts  29.2 us (7%)
  between operations  16.2 us (4%)
  other arithmetic  10.6 us (2%)
    reduce_scatter x1, waiting for transfers between devices, on_device(): lax.psum_scatter(lax.dot_general(gated_grad, image_attn, (((0,), (0,)), (...  168 us
    unnamed x2, blocking collectives  87.4 us
    all_gather x1, waiting for transfers between devices, on_device(): lax.all_gather(key_rows, 'seq', axis=0, tiled=True)  40.8 us
    reduce_scatter x1, waiting for transfers between devices, on_device(): lax.psum_scatter(partial_proj, 'seq', scatter_dimension=0, tiled=True)  32.1 us
    all_gather x1, waiting for transfers between devices, on_device(): lax.all_gather(value_rows, 'seq', axis=0, tiled=True)  24.5 us
    dot_general x1, matrix products, attend(): jnp.einsum('hqk,khd->hqd', weights_now.astype(jnp.bfloat16), value_heads,...  10.4 us
    all_gather x1, local copies, waits for them, and re-layouts, on_device(): lax.all_gather(value_rows, 'seq', axis=0, tiled=True)  9.37 us
    all_gather x1, local copies, waits for them, and re-layouts, on_device(): lax.all_gather(key_rows, 'seq', axis=0, tiled=True)  9.33 us
  transfers between devices with their start and end apart: 4, of which 4 were waited for; matrix products, arithmetic and copies ran while one was open for 8% of the time, Pallas kernels for 0%

commit v1 on v0

--- a/solution.py
+++ b/solution.py
@@ -106,7 +106,9 @@
     running = attend(
         start_state(query_heads),
         query_heads,
-        lax.all_gather(key_rows, "seq", axis=0, tiled=True),
+        jnp.concatenate(
+            lax.all_to_all(jnp.stack([key_rows] * lax.axis_size("seq")), "seq", 0, 0), axis=0
+        ),
         lax.all_gather(value_rows, "seq", axis=0, tiled=True),
         usable_all,
     )

time: 447 us -> 512 us (1.15)
  waiting for transfers between devices: 265 us -> 318 us
  local copies, waits for them, and re-layouts: 29.2 us -> 35.4 us
    all_to_all x0 -> x1, waiting for transfers between devices: none -> 116 us  [on_device(): lax.all_to_all(jnp.stack([key_rows] * lax.axis_size('seq')), 'seq', 0, 0)]
    all_gather x1 -> x0, waiting for transfers between devices: 40.8 us -> none  [on_device(): lax.all_gather(key_rows, 'seq', axis=0, tiled=True)]
    all_gather x1, waiting for transfers between devices: 24.5 us -> 0.02 us  [on_device(): lax.all_gather(value_rows, 'seq', axis=0, tiled=True)]
    another operation x0 -> x2, local copies, waits for them, and re-layouts: none -> 16.2 us  [the longest x1 13 us: attend(): key_heads = key_rows.reshape(count_keys, -1, head_size)]
    all_gather x1 -> x0, local copies, waits for them, and re-layouts: 9.33 us -> none  [on_device(): lax.all_gather(key_rows, 'seq', axis=0, tiled=True)]
  transfers between devices with their start and end apart: 4 -> 4, of which waited for: 4 -> 3; matrix products, arithmetic and copies ran while one was open for 8% -> 9% of each run, Pallas kernels for 0% -> 0%
where the time goes in v1:
time: 512 us; the launch traced here: 511 us
  waiting for transfers between devices  318 us (62%)
  blocking collectives  84.6 us (17%)
  matrix products  41.7 us (8%)
  local copies, waits for them, and re-layouts  35.4 us (7%)
  between operations  16.2 us (3%)
  other arithmetic  9.78 us (2%)
    reduce_scatter x1, waiting for transfers between devices, on_device(): lax.psum_scatter(lax.dot_general(gated_grad, image_attn, (((0,), (0,)), (...  169 us
    all_to_all x1, waiting for transfers between devices, on_device(): lax.all_to_all(jnp.stack([key_rows] * lax.axis_size('seq')), 'seq', 0, 0)  116 us
    unnamed x2, blocking collectives  84.6 us
    reduce_scatter x1, waiting for transfers between devices, on_device(): lax.psum_scatter(partial_proj, 'seq', scatter_dimension=0, tiled=True)  32.8 us
    another operation x1, local copies, waits for them, and re-layouts, attend(): key_heads = key_rows.reshape(count_keys, -1, head_size)  13 us
    dot_general x1, matrix products, attend(): jnp.einsum('hqk,khd->hqd', weights_now.astype(jnp.bfloat16), value_heads,...  10.4 us
  transfers between devices with their start and end apart: 4, of which 3 were waited for; matrix products, arithmetic and copies ran while one was open for 9% of the time, Pallas kernels for 0%

profile of v1, /device:TPU:0, one launch (start us, length us, event | category | flops | bytes accessed | tf_op | source)
XLA Modules:
  0.0 510.6 jit_solution(6823447556282568487)
XLA Ops:
  8.1 0.7 fusion.39
  8.7 0.7 bitcast_compare_fusion
  9.4 1.6 gather_fusion
  11.0 2.6 fusion.29
  13.7 1.2 dynamic-slice
  15.8 31.7 %all-reduce.1 = f32[128]{0:T(128)S(1)} all-reduce(f32[128]{0:T(128)S(1)} %fusion.28), channel_id=3, replica_groups=mesh['dp'=8,'seq'=16] {'seq'}, use_global_device_ids=true, to_apply=%region_2.3.clone | all-reduce | flops 128 | bytes 1024
  47.6 32.8 %reduce-scatter.3.cloned.1.call-done = f32[8,4608]{1,0:T(8,128)} async-done(((f32[128,4608]{1,0:T(8,128)}), f32[8,4608]{1,0:T(8,128)}) %reduce-scatter.3.cloned.1.call-update) | async-done | bytes 147472 | tf_op jit(solution)/shard_map/reduce_scatter | solution.py:89
  80.3 1.0 broadcast_multiply_fusion
  81.3 1.8 pad_maximum_fusion.1
  83.5 3.2 stack.2
  86.7 4.7 all-to-all-start
  92.1 116.4 %all-to-all-done = bf16[16,136,1536]{2,1,0:T(8,128)(2,1)} async-done(((bf16[16,136,1536]{2,1,0:T(8,128)(2,1)}), bf16[16,136,1536]{2,1,0:T(8,128)(2,1)}, u32[]{:S(2)}, u32[]{:S(2)}) %all-to-all-start) | async-done | bytes 6684704 | tf_op jit(solution)/shard_map/all_to_all | solution.py:110
  208.6 13.0 %reshape_reshape.3 = bf16[2176,12,128]{2,1,0:T(8,128)(2,1)} reshape(bf16[16,136,1536]{2,1,0:T(8,128)(2,1)} %all-to-all-done) | data formatting | bytes 13369344 | tf_op jit(solution)/shard_map/reshape;reshape | solution.py:41
  221.6 9.0 %fusion = (f32[12,136]{1,0:T(8,128)S(1)}, f32[12,136,2176]{2,1,0:T(8,128)S(1)}) fusion(pred[2176]{0:T(1024)(128)(4,1)S(1)} %broadcast_in_dim.67, bf16[2176,12,128]{2,1,0:T(8,128)(2,1)} %reshape_reshape.3, bf16[8,12,128]{2,0,1:T(8,128)(2,1)S(1)} %get-tuple-element.9, bf16[128,12,128]{2,0,1:T(8,128)(2,1)S(1)} %copy.26), kind=kOutput, calls=%fused_computation.3 | convolution fusion | flops 920603008 | bytes 21316096 | tf_op jit(solution)/shard_map/qhd,khd->hqk/dot_general | solution.py:43
  230.6 5.0 copy-done.2
  235.6 3.8 fusion.1
  239.4 9.4 %copy.28 = bf16[2176,1536]{0,1:T(8,128)(2,1)} copy(bf16[2176,1536]{1,0:T(8,128)(2,1)} %all-gather.2.cloned.1.call-done) | data formatting | bytes 13369344 | tf_op jit(solution)/shard_map/all_gather | solution.py:112
  248.8 10.4 %fusion.17 = bf16[136,12,128]{2,0,1:T(8,128)(2,1)S(1)} fusion(bf16[2176,12,128]{0,2,1:T(8,128)(2,1)} %bitcast.76, f32[12,136,2176]{2,1,0:T(8,128)} %copy-done.2, f32[12,136]{1,0:T(8,128)S(1)} %broadcast_maximum_fusion, pred[2176]{0:T(1024)(128)(4,1)S(1)} %broadcast_in_dim.67, f32[136,12]{0,1:T(8,128)S(1)} %bitcast.86), kind=kOutput, calls=%fused_computation.19 | convolution fusion | flops 927289344 | bytes 21322624 | tf_op jit(solution)/shard_map/hqk,khd->hqd/dot_general | solution.py:50
  259.6 8.1 %fusion.21 = f32[3072,1536]{1,0:T(8,128)} fusion(bf16[128,1536]{0,1:T(8,128)(2,1)S(1)} %bitcast.78, bf16[1,128,3072]{2,1,0:T(8,128)(2,1)S(1)} %copy-done.3, f32[3072]{0:T(1024)S(1)} %bitcast.81), kind=kOutput, calls=%fused_computation.21 | convolution fusion | flops 1209139200 | bytes 20066304 | tf_op jit(solution)/shard_map/dot_general | solution.py:135
  268.6 6.2 %fusion.8 = bf16[1,128,1536]{2,1,0:T(8,128)(2,1)} fusion(bf16[3072,1536]{1,0:T(8,128)(2,1)} %param.23, bf16[1,128,3072]{2,1,0:T(8,128)(2,1)} %param.25, f32[3072]{0:T(1024)S(1)} %bitcast.82), kind=kOutput, calls=%fused_computation.11 | convolution fusion | flops 1209335808 | bytes 10629120 | tf_op jit(solution)/shard_map/dot_general | solution.py:131
  275.0 5.4 %fusion.10 = (f32[3072]{0:T(1024)S(1)}, bf16[1,128,3072]{2,1,0:T(8,128)(2,1)}) fusion(bf16[1,128,3072]{2,1,0:T(8,128)(2,1)} %param.25, f32[3072]{0:T(1024)S(1)} %bitcast.83, bf16[128,1536]{0,1:T(8,128)(2,1)} %bitcast.79, bf16[3072,1536]{1,0:T(8,128)(2,1)S(1)} %bitcast.75), kind=kOutput, calls=%fused_computation.15 | convolution fusion | flops 1209922560 | bytes 11427840 | tf_op jit(solution)/shard_map/dot_general | solution.py:123
  280.4 52.9 %all-reduce.2 = f32[3072]{0:T(1024)S(1)} all-reduce(f32[3072]{0:T(1024)S(1)} %get-tuple-element.7), channel_id=5, replica_groups=mesh['dp'=8,'seq'=16] {'seq'}, use_global_device_ids=true, to_apply=%region_9.10.clone | all-reduce | flops 3072 | bytes 24576
  333.9 1.4 fusion.38
  335.3 168.8 %reduce-scatter.5.cloned.1.call-done = f32[24,1536]{1,0:T(8,128)} async-done(((f32[3072,1536]{1,0:T(8,128)}), f32[24,1536]{1,0:T(8,128)}) %reduce-scatter.5.cloned.1.call-update) | async-done | bytes 147472 | tf_op jit(solution)/shard_map/reduce_scatter | solution.py:134
  (57 shorter events, 2.6 us)
Async XLA Ops:
  7.2 3.8 copy-start
  7.2 76.0 %copy-start.10 = (f32[128]{0:T(128)S(1)}, f32[128]{0:T(128)}, u32[]{:S(2)}) copy-start(f32[128]{0:T(128)} %param.18) | copy-start | bytes 1540
  7.2 76.0 %copy-start.9 = (f32[128]{0:T(128)S(1)}, f32[128]{0:T(128)}, u32[]{:S(2)}) copy-start(f32[128]{0:T(128)} %param.19) | copy-start | bytes 1540
  7.2 76.2 %copy-start.7 = (bf16[1,128,1536]{2,1,0:T(8,128)(2,1)S(1)}, bf16[1,128,1536]{2,1,0:T(8,128)(2,1)}, u32[]{:S(2)}) copy-start(bf16[1,128,1536]{2,1,0:T(8,128)(2,1)} %param.21) | copy-start | bytes 1179652
  7.2 73.1 %reduce-scatter.3.cloned.1.call-start = ((), (), s32[]{:S(2)}) async-start(), calls=%async_computation.3 | async-start | bytes 2506752 | tf_op jit(solution)/shard_map/reduce_scatter | solution.py:89
  13.6 225.8 %all-gather.2.cloned.1.call-start = ((), (), s32[]{:S(2)}) async-start(), calls=%async_computation.4 | async-start | bytes 7102464 | tf_op jit(solution)/shard_map/all_gather | solution.py:112
  83.4 7.9 %copy-start.11 = (s32[1,128]{1,0:T(1,128)S(1)}, s32[1,128]{1,0:T(1,128)}, u32[]{:S(2)}) copy-start(s32[1,128]{1,0:T(1,128)} %param.17) | copy-start | bytes 1540
  83.4 8.2 %copy-start.8 = (bf16[1,128,1536]{2,1,0:T(8,128)(2,1)S(1)}, bf16[1,128,1536]{2,1,0:T(8,128)(2,1)}, u32[]{:S(2)}) copy-start(bf16[1,128,1536]{2,1,0:T(8,128)(2,1)} %param.20) | copy-start | bytes 1179652
  86.7 121.9 %all-to-all-start = ((bf16[16,136,1536]{2,1,0:T(8,128)(2,1)}), bf16[16,136,1536]{2,1,0:T(8,128)(2,1)}, u32[]{:S(2)}, u32[]{:S(2)}) async-start(bf16[16,136,1536]{2,1,0:T(8,128)(2,1)} %stack.2), calls=%async_computation.1 | async-start | bytes 13369344 | tf_op jit(solution)/shard_map/all_to_all | solution.py:110
  91.3 412.8 %reduce-scatter.5.cloned.1.call-start = ((), (), s32[]{:S(2)}) async-start(), calls=%async_computation.5 | async-start | bytes 19021824 | tf_op jit(solution)/shard_map/reduce_scatter | solution.py:134
  230.6 5.1 copy-start.2
  248.8 10.7 %copy-start.3 = (bf16[1,128,3072]{2,1,0:T(8,128)(2,1)S(1)}, bf16[1,128,3072]{2,1,0:T(8,128)(2,1)}, u32[]{:S(2)}) copy-start(bf16[1,128,3072]{2,1,0:T(8,128)(2,1)} %param.25) | copy-start | bytes 2359300
  248.8 10.7 %copy-start.6 = (f32[1,3072]{1,0:T(1,128)S(1)}, f32[1,3072]{1,0:T(1,128)}, u32[]{:S(2)}) copy-start(f32[1,3072]{1,0:T(1,128)} %param.24) | copy-start | bytes 36868
  259.3 8.4 %copy-start.5 = (bf16[136,12,128]{2,0,1:T(8,128)(2,1)}, bf16[136,12,128]{2,0,1:T(8,128)(2,1)S(1)}, u32[]{:S(2)}) copy-start(bf16[136,12,128]{2,0,1:T(8,128)(2,1)S(1)} %fusion.17) | copy-start | bytes 1253380
  259.6 8.1 %copy-start.4 = (bf16[128,12,128]{0,2,1:T(8,128)(2,1)}, bf16[128,12,128]{0,2,1:T(8,128)(2,1)S(1)}, u32[]{:S(2)}) copy-start(bf16[128,12,128]{0,2,1:T(8,128)(2,1)S(1)} %copy.30) | copy-start | bytes 1179652
  267.7 7.1 %slice-start = ((s8[9437184]{0:T(1024)(128)(4,1)}), s8[1048576]{0:T(1024)(128)(4,1)S(1)}, s32[]{:S(2)}) async-start(s8[9437184]{0:T(1024)(128)(4,1)} %bitcast.74), calls=%async_computation.6 | async-start | bytes 2097152
  268.6 6.2 %slice-start.1 = ((s8[9437184]{0:T(1024)(128)(4,1)}), s8[4194304]{0:T(1024)(128)(4,1)S(1)}, s32[]{:S(2)}) async-start(s8[9437184]{0:T(1024)(128)(4,1)} %bitcast.74), calls=%async_computation.7 | async-start | bytes 8388608
  268.6 6.4 %slice-start.2 = ((s8[9437184]{0:T(1024)(128)(4,1)}), s8[4194304]{0:T(1024)(128)(4,1)S(1)}, s32[]{:S(2)}) async-start(s8[9437184]{0:T(1024)(128)(4,1)} %bitcast.74), calls=%async_computation.8 | async-start | bytes 8388608
  268.6 235.6 %copy-start.1 = (bf16[256,4608]{1,0:T(8,128)(2,1)S(1)}, bf16[256,4608]{1,0:T(8,128)(2,1)}, u32[]{:S(2)}) copy-start(bf16[256,4608]{1,0:T(8,128)(2,1)} %param.15) | copy-start | bytes 7077892
Sparse Core Ops, SparseCore 0:
  13.8 66.5 reduce-scatter.2
  83.3 117.0 all-gather.1
  267.8 236.2 reduce-scatter.4
